TPU v7x, 512 devices: a whole 4x8x8 slice. The times are simulated.
512 devices in a mesh: grp: 16 (over z, core), blk: 32 (over y, x).
Axes of the slice: x: 4, y: 8, z: 8, core: 2. Of those that a mesh axis runs over, the one named last changes fastest.
Arguments:
- integrals: bfloat16 [32, 2048, 2048], P('blk', None, 'grp'), as said below
- tile_mask: int32 [16, 16], replicated, may hold values from 0 to 1, as said below
- tile_owner: int32 [16], replicated, may hold values from 0 to 15, as said below
- occupied_tiles: bfloat16 [16384, 128], P(('grp', 'blk')), may hold values from -0.1875 to 0.1875
- occupied_offsets: int32 [8], replicated, may hold values from 0 to 15, as said below
- virtual_tiles: bfloat16 [16384, 128], P(('grp', 'blk')), may hold values from -0.1875 to 0.1875
- virtual_offsets: int32 [8], replicated, may hold values from 0 to 15, as said below
Outputs:
- polarizability: float32 [32, 32], P('blk')
Inputs may be any that keep to these rules, and one draw needn't show every extreme that they name: `integrals`: after column slot s is placed at basis tile tile_owner[s], the tensor is symmetric in its two basis indices. `tile_mask`: symmetric, with ones on the diagonal. `tile_owner`: each tile exactly once. `occupied_offsets`: 8 different tile offsets, among them 0 and 15. `virtual_offsets`: 8 different tile offsets, among them 0 and 15.
All inputs are finite; a program needn't handle non-finite values.
Results may differ from a plain program's by a relative error of at most 0.004.
Values may be sent and summed in bfloat16 or wider, within the bound.
A program may use at most 64 MiB of HBM per device.

v0:
```python
import jax
import jax.numpy as jnp
from jax import lax
from jax.sharding import PartitionSpec as P

NT = 16


def body(
    integrals,
    tile_mask,
    tile_owner,
    occupied_tiles,
    occupied_offsets,
    virtual_tiles,
    virtual_offsets,
):
    aux_local, basis_size, local_width = integrals.shape
    tile_width = basis_size // NT
    kcount = occupied_offsets.shape[0]
    local_tiles = local_width // tile_width
    group_index = lax.axis_index("grp")
    local_owner = lax.dynamic_slice_in_dim(tile_owner, group_index * local_tiles, local_tiles)
    matches = (local_owner[None, :, None] == jnp.arange(NT, dtype=jnp.int32)[None, None, :]).astype(
        jnp.int32
    )
    column_mask = jnp.sum(tile_mask[:, None, :] * matches, axis=2)
    blocked = integrals.reshape(aux_local, NT, tile_width, local_tiles, tile_width)
    masked = blocked * column_mask.astype(jnp.bfloat16)[None, :, None, :, None]
    masked = masked.reshape(aux_local, NT, tile_width, local_width)
    occupied_all, virtual_all = (
        lax.all_gather(occupied_tiles, ("grp", "blk"), axis=0, tiled=True),
        lax.all_gather(virtual_tiles, ("grp", "blk"), axis=0, tiled=True),
    )
    occupied_all = occupied_all.reshape(NT, kcount, tile_width, tile_width)
    virtual_all = virtual_all.reshape(NT, kcount, tile_width, tile_width)
    source_rows = (tile_owner[:, None] - occupied_offsets[None, :]) % NT
    partner_rows = (tile_owner[:, None] + virtual_offsets[None, :]) % NT
    virtual_pick = virtual_all[tile_owner]
    occupied_sum = jnp.zeros((aux_local, NT, tile_width, local_width), jnp.float32)
    virtual_sum = jnp.zeros((aux_local, local_width, NT, tile_width), jnp.float32)
    for slot in range(kcount):
        occupied_pick = occupied_all[source_rows[:, slot], slot]
        occupied_inputs = masked[:, source_rows[:, slot]]
        occupied_sum = occupied_sum + jnp.einsum(
            "tmn,ptml->ptnl", occupied_pick, occupied_inputs, preferred_element_type=jnp.float32
        )
        virtual_inputs = masked[:, partner_rows[:, slot]]
        virtual_sum = virtual_sum + jnp.einsum(
            "tnm,ptml->pltn",
            virtual_pick[:, slot],
            virtual_inputs,
            preferred_element_type=jnp.float32,
        )
    occupied_part = occupied_sum.astype(jnp.bfloat16)
    virtual_part = virtual_sum.astype(jnp.bfloat16).reshape(
        aux_local, local_tiles, tile_width, basis_size
    )
    occupied_moved = lax.all_to_all(occupied_part, "grp", split_axis=1, concat_axis=3, tiled=True)
    occupied_full, virtual_full = (
        lax.all_to_all(occupied_moved, "blk", split_axis=2, concat_axis=0, tiled=True),
        lax.all_to_all(virtual_part, "blk", split_axis=2, concat_axis=0, tiled=True),
    )
    left_side = occupied_full.reshape(occupied_full.shape[0], -1)
    right_side = virtual_full.reshape(virtual_full.shape[0], -1)
    partial_sum = jnp.einsum(
        "pe,qe->pq", left_side, right_side, preferred_element_type=jnp.float32
    ) * (1.0 / basis_size)
    total = lax.psum(partial_sum, ("grp", "blk"))
    return lax.dynamic_slice_in_dim(total, lax.axis_index("blk") * aux_local, aux_local, 0)


def solution(mesh):
    in_specs = (
        P("blk", None, "grp"),
        P(),
        P(),
        P(("grp", "blk"), None),
        P(),
        P(("grp", "blk"), None),
        P(),
    )
    out_specs = P("blk", None)
    return jax.shard_map(body, mesh=mesh, in_specs=in_specs, out_specs=out_specs, check_vma=False)
```

profile of v0, /device:TPU:1, one launch (start us, length us, event | category | flops | bytes accessed | tf_op | source)
XLA Modules:
  0.0 427.2 jit_solution(16286854891178512670)
XLA Ops:
  15.5 1.5 gather_fusion.19
  16.9 1.4 gather_fusion.20
  19.8 1.4 gather_fusion.22
  23.3 1.4 gather_fusion
  26.2 1.4 gather_fusion.4
  27.6 1.4 gather_fusion.6
  29.0 1.5 gather_fusion.8
  34.0 102.1 %all-gather.3.cloned.1.call-done = bf16[16384,128]{1,0:T(8,128)(2,1)} async-done(((bf16[32,128]{1,0:T(8,128)(2,1)}), bf16[16384,128]{1,0:T(8,128)(2,1)}) %all-gather.3.cloned.1.call-update) | async-done | bytes 4194320 | tf_op jit(solution)/shard_map/all_gather | solution.py:32
  136.1 3.6 gather_fusion.1
  139.7 3.6 gather_fusion.3
  143.3 3.6 gather_fusion.5
  146.9 3.6 gather_fusion.7
  150.5 2.9 gather_fusion.9
  153.4 2.8 gather_fusion.11
  156.2 2.8 gather_fusion.13
  159.1 2.8 gather_fusion.15
  162.0 1.7 fusion.25
  163.7 1.6 convolution_add_fusion.13
  168.3 6.0 %all-to-all-start = ((bf16[1,16,128,128]{2,3,0,1:T(8,128)(2,1)}), bf16[1,16,128,128]{2,3,0,1:T(8,128)(2,1)S(1)}, u32[]{:S(2)}, u32[]{:S(2)}) async-start(bf16[1,16,128,128]{2,3,0,1:T(8,128)(2,1)} %fusion.2), calls=%async_computation | async-start | bytes 1048576 | tf_op jit(solution)/shard_map/all_to_all | solution.py:59
  174.4 81.7 %all-gather.5.cloned.1.call-done = bf16[16384,128]{1,0:T(8,128)(2,1)} async-done(((bf16[32,128]{1,0:T(8,128)(2,1)}), bf16[16384,128]{1,0:T(8,128)(2,1)}) %all-gather.5.cloned.1.call-update) | async-done | bytes 4194320 | tf_op jit(solution)/shard_map/all_gather | solution.py:33
  256.1 5.4 %gather_fusion.17 = bf16[16,8,128,128]{3,2,1,0:T(8,128)(2,1)} fusion(bf16[16,8,128,128]{3,2,1,0:T(8,128)(2,1)} %bitcast.152, s32[1024]{0:T(1024)S(1)} %pad_clamp_fusion.8), kind=kCustom, calls=%fused_computation.17 | custom fusion | bytes 8388672 | tf_op jit(solution)/shard_map/gather | solution.py:39
  261.4 1.5 fusion.4
  262.9 1.6 convolution_add_fusion.6
  268.0 3.7 reduce.6
  272.9 6.9 %all-to-all-start.2 = ((bf16[32,2,4096]{2,1,0:T(2,128)(2,1)}), bf16[32,2,4096]{2,1,0:T(2,128)(2,1)S(1)}, u32[]{:S(2)}, u32[]{:S(2)}) async-start(bf16[32,2,4096]{2,1,0:T(2,128)(2,1)} %reshape.405), calls=%async_computation.2 | async-start | bytes 1048576 | tf_op jit(solution)/shard_map/all_to_all | solution.py:62
  280.7 3.7 reduce.7
  285.6 10.8 %all-to-all-done.2 = bf16[32,2,4096]{2,1,0:T(2,128)(2,1)S(1)} async-done(((bf16[32,2,4096]{2,1,0:T(2,128)(2,1)}), bf16[32,2,4096]{2,1,0:T(2,128)(2,1)S(1)}, u32[]{:S(2)}, u32[]{:S(2)}) %all-to-all-start.2) | async-done | bytes 524320 | tf_op jit(solution)/shard_map/all_to_all | solution.py:62
  296.4 5.2 %all-to-all-start.1 = ((bf16[32,2,4096]{2,1,0:T(2,128)(2,1)}), bf16[32,2,4096]{2,1,0:T(2,128)(2,1)S(1)}, u32[]{:S(2)}, u32[]{:S(2)}) async-start(bf16[32,2,4096]{2,1,0:T(2,128)(2,1)} %reshape.407), calls=%async_computation.1 | async-start | bytes 1048576 | tf_op jit(solution)/shard_map/all_to_all | solution.py:61
  302.2 3.0 bitcast_reduce_fusion.1
  305.4 11.3 %all-to-all-done.1 = bf16[32,2,4096]{2,1,0:T(2,128)(2,1)S(1)} async-done(((bf16[32,2,4096]{2,1,0:T(2,128)(2,1)}), bf16[32,2,4096]{2,1,0:T(2,128)(2,1)S(1)}, u32[]{:S(2)}, u32[]{:S(2)}) %all-to-all-start.1) | async-done | bytes 524320 | tf_op jit(solution)/shard_map/all_to_all | solution.py:61
  317.2 3.0 bitcast_reduce_fusion
  321.6 98.2 %psum.7 = f32[32,32]{1,0:T(8,128)S(1)} all-reduce(f32[32,32]{1,0:T(8,128)S(1)} %fusion.3), channel_id=1, replica_groups=mesh['grp'=16,'blk'=32] {'grp','blk'}, use_global_device_ids=true, to_apply=%region_1.2 | all-reduce | flops 1024 | bytes 8192 | tf_op jit(solution)/shard_map/psum | solution.py:69
  (87 shorter events, 30.2 us)
Async XLA Ops:
  6.5 129.6 %all-gather.3.cloned.1.call-start = ((), (), s32[]{:S(2)}) async-start(), calls=%async_computation.3 | async-start | bytes 4202496 | tf_op jit(solution)/shard_map/all_gather | solution.py:32
  7.3 248.8 %all-gather.5.cloned.1.call-start = ((), (), s32[]{:S(2)}) async-start(), calls=%async_computation.4 | async-start | bytes 4202496 | tf_op jit(solution)/shard_map/all_gather | solution.py:33
  23.3 10.7 %copy-start.15 = (s32[16]{0:T(128)S(1)}, s32[16]{0:T(128)}, u32[]{:S(2)}) copy-start(s32[16]{0:T(128)} %param.9) | copy-start | bytes 196
  161.9 3.4 copy-start.2
  161.9 3.4 copy-start.11
  161.9 3.7 copy-start.1
  161.9 3.7 copy-start.10
  163.7 2.4 copy-start.13
  165.3 1.1 copy-start.12
  165.7 1.1 copy-start.14
  168.3 104.6 %all-to-all-start = ((bf16[1,16,128,128]{2,3,0,1:T(8,128)(2,1)}), bf16[1,16,128,128]{2,3,0,1:T(8,128)(2,1)S(1)}, u32[]{:S(2)}, u32[]{:S(2)}) async-start(bf16[1,16,128,128]{2,3,0,1:T(8,128)(2,1)} %fusion.2), calls=%async_computation | async-start | bytes 1048576 | tf_op jit(solution)/shard_map/all_to_all | solution.py:59
  256.1 5.4 %copy-start.3 = (bf16[16,128,128]{2,1,0:T(8,128)(2,1)S(1)}, bf16[16,128,128]{2,1,0:T(8,128)(2,1)}, u32[]{:S(2)}) copy-start(bf16[16,128,128]{2,1,0:T(8,128)(2,1)} %gather_fusion.16) | copy-start | bytes 1572868
  256.1 6.9 %copy-start.4 = (bf16[16,128,128]{2,1,0:T(8,128)(2,1)S(1)}, bf16[16,128,128]{2,1,0:T(8,128)(2,1)}, u32[]{:S(2)}) copy-start(bf16[16,128,128]{2,1,0:T(8,128)(2,1)} %gather_fusion.18) | copy-start | bytes 1572868
  261.4 3.1 copy-start
  261.4 3.1 copy-start.5
  261.4 3.4 copy-start.6
  262.9 2.2 copy-start.7
  264.5 1.1 copy-start.8
  264.8 1.1 copy-start.9
  272.9 23.5 %all-to-all-start.2 = ((bf16[32,2,4096]{2,1,0:T(2,128)(2,1)}), bf16[32,2,4096]{2,1,0:T(2,128)(2,1)S(1)}, u32[]{:S(2)}, u32[]{:S(2)}) async-start(bf16[32,2,4096]{2,1,0:T(2,128)(2,1)} %reshape.405), calls=%async_computation.2 | async-start | bytes 1048576 | tf_op jit(solution)/shard_map/all_to_all | solution.py:62
  296.4 20.3 %all-to-all-start.1 = ((bf16[32,2,4096]{2,1,0:T(2,128)(2,1)}), bf16[32,2,4096]{2,1,0:T(2,128)(2,1)S(1)}, u32[]{:S(2)}, u32[]{:S(2)}) async-start(bf16[32,2,4096]{2,1,0:T(2,128)(2,1)} %reshape.407), calls=%async_computation.1 | async-start | bytes 1048576 | tf_op jit(solution)/shard_map/all_to_all | solution.py:61
Sparse Core Ops, SparseCore 0:
  11.5 124.5 all-gather.2
  140.3 115.6 all-gather.4
where the time goes:
time: 428 us; the launch traced here: 427 us
  waiting for transfers between devices  207 us (48%)
  blocking collectives  98.2 us (23%)
  local copies, waits for them, and re-layouts  66.5 us (16%)
  starting transfers between devices  18.1 us (4%)
  between operations  13.9 us (3%)
  matrix products  12.2 us (3%)
  other arithmetic  10.9 us (3%)
    all_gather x1, waiting for transfers between devices, body(): lax.all_gather(occupied_tiles, ('grp', 'blk'), axis=0, tiled=True)  102 us
    psum x1, blocking collectives, body(): total = lax.psum(partial_sum, ('grp', 'blk'))  98.2 us
    all_gather x1, waiting for transfers between devices, body(): lax.all_gather(virtual_tiles, ('grp', 'blk'), axis=0, tiled=True)  81.7 us
    gather x8, local copies, waits for them, and re-layouts, body(): occupied_pick = occupied_all[source_rows[:, slot], slot]  25.8 us
    all_to_all x1, waiting for transfers between devices, body(): lax.all_to_all(occupied_moved, 'blk', split_axis=2, concat_axis=0, tiled=...  11.3 us
    all_to_all x1, waiting for transfers between devices, body(): lax.all_to_all(virtual_part, 'blk', split_axis=2, concat_axis=0, tiled=True)  10.8 us
    gather x8, local copies, waits for them, and re-layouts, body(): occupied_inputs = masked[:, source_rows[:, slot]]  10.6 us
    gather x8, local copies, waits for them, and re-layouts, body(): virtual_inputs = masked[:, partner_rows[:, slot]]  10.6 us
  transfers between devices with their start and end apart: 5, of which 4 were waited for; matrix products, arithmetic and copies ran while one was open for 20% of the time, Pallas kernels for 0%

commit v1 on v0

--- a/solution.py
+++ b/solution.py
@@ -66,7 +66,7 @@
     partial_sum = jnp.einsum(
         "pe,qe->pq", left_side, right_side, preferred_element_type=jnp.float32
     ) * (1.0 / basis_size)
-    total = lax.psum(partial_sum, ("grp", "blk"))
+    total = jnp.sum(lax.all_gather(partial_sum, ("grp", "blk")), axis=0)
     return lax.dynamic_slice_in_dim(total, lax.axis_index("blk") * aux_local, aux_local, 0)
 
 

time: 428 us -> 459 us (1.072)
  waiting for transfers between devices: 207 us -> 332 us
  blocking collectives: 98.2 us -> 0 us
    all_gather x0 -> x1, waiting for transfers between devices: none -> 125 us  [body(): total = jnp.sum(lax.all_gather(partial_sum, ('grp', 'blk')), axis=0)]
    psum x1 -> x0, blocking collectives: 98.2 us -> none  [body(): total = lax.psum(partial_sum, ('grp', 'blk'))]
  transfers between devices with their start and end apart: 5 -> 6, of which waited for: 4 -> 5; matrix products, arithmetic and copies ran while one was open for 20% -> 18% of each run, Pallas kernels for 0% -> 0%
where the time goes in v1:
time: 459 us; the launch traced here: 458 us
  waiting for transfers between devices  332 us (72%)
  local copies, waits for them, and re-layouts  66.6 us (15%)
  starting transfers between devices  18.2 us (4%)
  other arithmetic  14.9 us (3%)
  between operations  13.6 us (3%)
  matrix products  12.8 us (3%)
    all_gather x1, waiting for transfers between devices, body(): total = jnp.sum(lax.all_gather(partial_sum, ('grp', 'blk')), axis=0)  125 us
    all_gather x1, waiting for transfers between devices, body(): lax.all_gather(occupied_tiles, ('grp', 'blk'), axis=0, tiled=True)  102 us
    all_gather x1, waiting for transfers between devices, body(): lax.all_gather(virtual_tiles, ('grp', 'blk'), axis=0, tiled=True)  81.7 us
    gather x8, local copies, waits for them, and re-layouts, body(): occupied_pick = occupied_all[source_rows[:, slot], slot]  25.8 us
    all_to_all x1, waiting for transfers between devices, body(): lax.all_to_all(occupied_moved, 'blk', split_axis=2, concat_axis=0, tiled=...  11.3 us
    all_to_all x1, waiting for transfers between devices, body(): lax.all_to_all(virtual_part, 'blk', split_axis=2, concat_axis=0, tiled=True)  10.8 us
    gather x8, local copies, waits for them, and re-layouts, body(): occupied_inputs = masked[:, source_rows[:, slot]]  10.6 us
    gather x8, local copies, waits for them, and re-layouts, body(): virtual_inputs = masked[:, partner_rows[:, slot]]  10.6 us
  transfers between devices with their start and end apart: 6, of which 5 were waited for; matrix products, arithmetic and copies ran while one was open for 18% of the time, Pallas kernels for 0%

profile of v1, /device:TPU:1, one launch (start us, length us, event | category | flops | bytes accessed | tf_op | source)
XLA Modules:
  0.0 458.1 jit_solution(11678950308730475279)
XLA Ops:
  15.5 1.5 gather_fusion.19
  19.8 1.4 gather_fusion.22
  23.4 1.4 gather_fusion
  26.2 1.4 gather_fusion.4
  29.1 1.5 gather_fusion.8
  34.0 102.1 %all-gather.5.cloned.1.call-done = bf16[16384,128]{1,0:T(8,128)(2,1)} async-done(((bf16[32,128]{1,0:T(8,128)(2,1)}), bf16[16384,128]{1,0:T(8,128)(2,1)}) %all-gather.5.cloned.1.call-update) | async-done | bytes 4194320 | tf_op jit(solution)/shard_map/all_gather | solution.py:32
  136.1 3.6 gather_fusion.1
  139.7 3.6 gather_fusion.3
  143.3 3.6 gather_fusion.5
  146.9 3.6 gather_fusion.7
  150.5 2.9 gather_fusion.9
  153.4 2.8 gather_fusion.11
  156.2 2.8 gather_fusion.13
  159.1 2.8 gather_fusion.15
  162.0 1.7 fusion.25
  163.7 1.6 convolution_add_fusion.13
  168.3 6.0 %all-to-all-start = ((bf16[1,16,128,128]{2,3,0,1:T(8,128)(2,1)}), bf16[1,16,128,128]{2,3,0,1:T(8,128)(2,1)S(1)}, u32[]{:S(2)}, u32[]{:S(2)}) async-start(bf16[1,16,128,128]{2,3,0,1:T(8,128)(2,1)} %fusion.2), calls=%async_computation | async-start | bytes 1048576 | tf_op jit(solution)/shard_map/all_to_all | solution.py:59
  174.4 81.7 %all-gather.7.cloned.1.call-done = bf16[16384,128]{1,0:T(8,128)(2,1)} async-done(((bf16[32,128]{1,0:T(8,128)(2,1)}), bf16[16384,128]{1,0:T(8,128)(2,1)}) %all-gather.7.cloned.1.call-update) | async-done | bytes 4194320 | tf_op jit(solution)/shard_map/all_gather | solution.py:33
  256.1 5.4 %gather_fusion.17 = bf16[16,8,128,128]{3,2,1,0:T(8,128)(2,1)} fusion(bf16[16,8,128,128]{3,2,1,0:T(8,128)(2,1)} %bitcast.154, s32[1024]{0:T(1024)S(1)} %pad_clamp_fusion.8), kind=kCustom, calls=%fused_computation.17 | custom fusion | bytes 8388672 | tf_op jit(solution)/shard_map/gather | solution.py:39
  261.4 1.5 fusion.4
  262.9 1.6 convolution_add_fusion.6
  268.0 3.7 reduce.6
  272.9 6.9 %all-to-all-start.2 = ((bf16[32,2,4096]{2,1,0:T(2,128)(2,1)}), bf16[32,2,4096]{2,1,0:T(2,128)(2,1)S(1)}, u32[]{:S(2)}, u32[]{:S(2)}) async-start(bf16[32,2,4096]{2,1,0:T(2,128)(2,1)} %reshape.406), calls=%async_computation.2 | async-start | bytes 1048576 | tf_op jit(solution)/shard_map/all_to_all | solution.py:62
  280.7 3.7 reduce.7
  285.7 10.8 %all-to-all-done.2 = bf16[32,2,4096]{2,1,0:T(2,128)(2,1)S(1)} async-done(((bf16[32,2,4096]{2,1,0:T(2,128)(2,1)}), bf16[32,2,4096]{2,1,0:T(2,128)(2,1)S(1)}, u32[]{:S(2)}, u32[]{:S(2)}) %all-to-all-start.2) | async-done | bytes 524320 | tf_op jit(solution)/shard_map/all_to_all | solution.py:62
  296.4 5.0 %all-to-all-start.1 = ((bf16[32,2,4096]{2,1,0:T(2,128)(2,1)}), bf16[32,2,4096]{2,1,0:T(2,128)(2,1)S(1)}, u32[]{:S(2)}, u32[]{:S(2)}) async-start(bf16[32,2,4096]{2,1,0:T(2,128)(2,1)} %reshape.408), calls=%async_computation.1 | async-start | bytes 1048576 | tf_op jit(solution)/shard_map/all_to_all | solution.py:61
  302.2 3.0 bitcast_reduce_fusion.1
  305.4 11.3 %all-to-all-done.1 = bf16[32,2,4096]{2,1,0:T(2,128)(2,1)S(1)} async-done(((bf16[32,2,4096]{2,1,0:T(2,128)(2,1)}), bf16[32,2,4096]{2,1,0:T(2,128)(2,1)S(1)}, u32[]{:S(2)}, u32[]{:S(2)}) %all-to-all-start.1) | async-done | bytes 524320 | tf_op jit(solution)/shard_map/all_to_all | solution.py:61
  317.2 3.0 bitcast_reduce_fusion
  320.4 1.8 fusion.3
  322.3 124.8 %all-gather.9.cloned.1.call-done = f32[16384,32]{1,0:T(8,128)} async-done(((f32[32,32]{1,0:T(8,128)}), f32[16384,32]{1,0:T(8,128)}) %all-gather.9.cloned.1.call-update) | async-done | bytes 2097168 | tf_op jit(solution)/shard_map/all_gather | solution.py:69
  447.1 4.0 reduce_sum.19
  (90 shorter events, 32.1 us)
Async XLA Ops:
  6.5 129.6 %all-gather.5.cloned.1.call-start = ((), (), s32[]{:S(2)}) async-start(), calls=%async_computation.3 | async-start | bytes 4202496 | tf_op jit(solution)/shard_map/all_gather | solution.py:32
  7.3 248.8 %all-gather.7.cloned.1.call-start = ((), (), s32[]{:S(2)}) async-start(), calls=%async_computation.4 | async-start | bytes 4202496 | tf_op jit(solution)/shard_map/all_gather | solution.py:33
  23.3 10.6 %copy-start.15 = (s32[16]{0:T(128)S(1)}, s32[16]{0:T(128)}, u32[]{:S(2)}) copy-start(s32[16]{0:T(128)} %param.9) | copy-start | bytes 196
  161.9 3.4 copy-start.2
  161.9 3.4 copy-start.11
  161.9 3.7 copy-start.1
  162.0 3.7 copy-start.10
  163.7 2.4 copy-start.13
  165.3 1.1 copy-start.12
  165.7 1.1 copy-start.14
  168.3 104.6 %all-to-all-start = ((bf16[1,16,128,128]{2,3,0,1:T(8,128)(2,1)}), bf16[1,16,128,128]{2,3,0,1:T(8,128)(2,1)S(1)}, u32[]{:S(2)}, u32[]{:S(2)}) async-start(bf16[1,16,128,128]{2,3,0,1:T(8,128)(2,1)} %fusion.2), calls=%async_computation | async-start | bytes 1048576 | tf_op jit(solution)/shard_map/all_to_all | solution.py:59
  256.1 5.4 %copy-start.3 = (bf16[16,128,128]{2,1,0:T(8,128)(2,1)S(1)}, bf16[16,128,128]{2,1,0:T(8,128)(2,1)}, u32[]{:S(2)}) copy-start(bf16[16,128,128]{2,1,0:T(8,128)(2,1)} %gather_fusion.16) | copy-start | bytes 1572868
  256.1 6.9 %copy-start.4 = (bf16[16,128,128]{2,1,0:T(8,128)(2,1)S(1)}, bf16[16,128,128]{2,1,0:T(8,128)(2,1)}, u32[]{:S(2)}) copy-start(bf16[16,128,128]{2,1,0:T(8,128)(2,1)} %gather_fusion.18) | copy-start | bytes 1572868
  261.4 3.1 copy-start
  261.4 3.1 copy-start.5
  261.4 3.4 copy-start.6
  262.9 2.2 copy-start.7
  264.5 1.1 copy-start.8
  264.9 1.1 copy-start.9
  272.9 23.5 %all-to-all-start.2 = ((bf16[32,2,4096]{2,1,0:T(2,128)(2,1)}), bf16[32,2,4096]{2,1,0:T(2,128)(2,1)S(1)}, u32[]{:S(2)}, u32[]{:S(2)}) async-start(bf16[32,2,4096]{2,1,0:T(2,128)(2,1)} %reshape.406), calls=%async_computation.2 | async-start | bytes 1048576 | tf_op jit(solution)/shard_map/all_to_all | solution.py:62
  296.4 20.3 %all-to-all-start.1 = ((bf16[32,2,4096]{2,1,0:T(2,128)(2,1)}), bf16[32,2,4096]{2,1,0:T(2,128)(2,1)S(1)}, u32[]{:S(2)}, u32[]{:S(2)}) async-start(bf16[32,2,4096]{2,1,0:T(2,128)(2,1)} %reshape.408), calls=%async_computation.1 | async-start | bytes 1048576 | tf_op jit(solution)/shard_map/all_to_all | solution.py:61
  301.4 145.7 %all-gather.9.cloned.1.call-start = ((), (), s32[]{:S(2)}) async-start(), calls=%async_computation.5 | async-start | bytes 8404992 | tf_op jit(solution)/shard_map/all_gather | solution.py:69
Sparse Core Ops, SparseCore 0:
  11.5 124.5 all-gather.4
  140.3 115.7 all-gather.6
  322.4 124.6 all-gather.8
